TPU v7x, 32 devices: a whole 2x2x4 slice. The times are simulated.
32 devices in a mesh: cells: 8 (over y, x, core), obs: 4 (over z).
Axes of the slice: x: 2, y: 2, z: 4, core: 2. Of those that a mesh axis runs over, the one named last changes fastest.
Arguments:
- histories: bfloat16 [64, 384], P('obs'), may hold values from -6 to 6
- amplitude: bfloat16 [64, 5, 8192], P('obs', None, 'cells'), may hold values from -0.75 to 0.75
- weights: bfloat16 [8192, 256], P('cells'), may hold values from -0.375 to 0.375
- retarded: int32 [64, 64], P('obs', 'cells'), may hold values from 0 to 128
- owner_block: int32 [8192], P('cells'), may hold values from 0 to 7, as said below
- owner_cell: int32 [8192], P('cells'), may hold values from 0 to 16383
- adjoint: float32 [5, 16, 64, 128], P(None, 'cells', 'obs'), may hold values from -6 to 6
- step_size: float32 [16, 64, 128], P('cells', 'obs'), may hold values from 0.1 to 0.6
- jacobian: float32 [8, 3, 5, 5], P('cells'), may hold values from -6 to 6
Outputs:
- adjoint_next: float32 [5, 16, 64, 128], P(None, 'cells', 'obs')
- panel_source: float32 [5, 8192], P(None, 'cells')
Inputs may be any that keep to these rules, and one draw needn't show every extreme that they name: `owner_block`: among each device's 1024 panels at most 512 name one owner block; one owner block, drawn from the seed, is named by exactly 512 panels of every device.
All inputs are finite; a program needn't handle non-finite values.
Results may differ from a plain program's by a relative error of at most 0.0003.
Values sent between devices are 32-bit elements; how exact they have to be, the bound alone decides.
A program may use at most 192 MiB of HBM per device.

v0:
```python
import jax
import jax.numpy as jnp
from jax import lax
from jax.sharding import PartitionSpec as P

SAMPLES = 256
SPAN = 128
COMP = 5
TILE = 128
smoothing = 0.25


def extended(cells, sides, width, closed):
    for axis, dim in sides:
        count = lax.axis_size(axis)
        ends = count if closed else count - 1
        head = lax.slice_in_dim(cells, 0, width, axis=dim)
        tail = lax.slice_in_dim(cells, cells.shape[dim] - width, cells.shape[dim], axis=dim)
        cells = jnp.concatenate(
            [
                lax.ppermute(tail, axis, [(i, (i + 1) % count) for i in range(ends)]),
                cells,
                lax.ppermute(head, axis, [((i + 1) % count, i) for i in range(ends)]),
            ],
            axis=dim,
        )
    return cells


def on_device(
    histories, amplitude, weights, retarded, owner_block, owner_cell, adjoint, step_size, jacobian
):
    tile_count = weights.shape[0] // TILE
    weights_tiled = weights.reshape(tile_count, TILE, SAMPLES)
    observers_local = histories.shape[0]
    history_len = histories.shape[1]
    shifted = jnp.broadcast_to(histories[:, None, :], (observers_local, tile_count, history_len))
    for bit_number in range(SPAN.bit_length()):
        amount = 1 << bit_number
        moved = jnp.concatenate(
            [
                shifted[..., amount:],
                jnp.zeros((observers_local, tile_count, amount), shifted.dtype),
            ],
            axis=2,
        )
        chosen = retarded >> bit_number & 1 == 1
        shifted = jnp.where(chosen[:, :, None], moved, shifted)
    window = shifted[..., :SAMPLES]
    projected = jnp.einsum(
        "tps,ots->otp", weights_tiled, window, preferred_element_type=jnp.float32
    )
    projected = projected.reshape(projected.shape[0], -1)
    partial_value = jnp.sum(amplitude.astype(jnp.float32) * projected[:, None, :], axis=0)
    panel_source = lax.psum(partial_value, "obs")
    my_block = lax.axis_index("cells")
    my_group = lax.axis_index("obs")
    azimuth_local = adjoint.shape[1]
    radial_local = adjoint.shape[2]
    axial_len = adjoint.shape[3]
    radial_all = radial_local * lax.axis_size("obs")
    block_cells = azimuth_local * radial_all * axial_len
    device_cells = azimuth_local * radial_local * axial_len
    target = (owner_block * block_cells + owner_cell).reshape(1, -1)
    empty_field = jnp.zeros((COMP, device_cells), jnp.float32)
    devices = lax.axis_size("cells")
    capacity = 4 * owner_block.shape[0] // devices
    one_hot = (owner_block[:, None] == jnp.arange(devices, dtype=jnp.int32)[None, :]).astype(
        jnp.int32
    )
    slot_rank = jnp.sum(jnp.cumsum(one_hot, axis=0) * one_hot, axis=1) - 1
    slot_of = owner_block * capacity + slot_rank
    outgoing = jnp.zeros((COMP, devices * capacity), jnp.float32).at[:, slot_of].set(panel_source)
    out_index = jnp.full((1, devices * capacity), -1, jnp.int32).at[0, slot_of].set(target[0])
    received, arrivals = (
        lax.all_to_all(outgoing, "cells", split_axis=1, concat_axis=1, tiled=True),
        lax.all_to_all(out_index, "cells", split_axis=1, concat_axis=1, tiled=True),
    )
    flat_index = arrivals[0]
    block_of = flat_index // block_cells
    within = flat_index % block_cells
    azimuth = within // (radial_all * axial_len)
    radius = within // axial_len % radial_all
    axial = within % axial_len
    is_mine = (block_of == my_block) & (radius // radial_local == my_group) & (flat_index >= 0)
    position = (azimuth * radial_local + radius - my_group * radial_local) * axial_len + axial
    landing = jnp.where(is_mine, position, device_cells)
    surface = empty_field.at[:, landing].add(received, mode="drop")
    widened = extended(adjoint, (("cells", 1),), 1, True)
    heightened = extended(adjoint, (("obs", 2),), 1, False)
    deepened = jnp.pad(adjoint, ((0, 0), (0, 0), (0, 0), (1, 1)))
    matrices = jacobian[0]
    neighbours = (
        (widened[:, 2:], widened[:, :-2]),
        (heightened[:, :, 2:], heightened[:, :, :-2]),
        (deepened[..., 2:], deepened[..., :-2]),
    )
    summed = jnp.zeros_like(adjoint)
    for direction in range(3):
        forward, backward = neighbours[direction]
        rotated = jnp.einsum(
            "kc,karz->carz",
            matrices[direction],
            forward - backward,
            precision=lax.Precision.HIGHEST,
        )
        summed = summed + (0.5 * rotated + smoothing * (forward - 2.0 * adjoint + backward))
    adjoint_next = adjoint + step_size[None] * summed + surface.reshape(adjoint.shape)
    return (adjoint_next, panel_source)


def solution(mesh):
    return jax.shard_map(
        on_device,
        mesh=mesh,
        in_specs=(
            P("obs", None),
            P("obs", None, "cells"),
            P("cells", None),
            P("obs", "cells"),
            P("cells"),
            P("cells"),
            P(None, "cells", "obs", None),
            P("cells", "obs", None),
            P("cells", None, None, None),
        ),
        out_specs=(P(None, "cells", "obs", None), P(None, "cells")),
        check_vma=False,
    )
```

profile of v0, /device:TPU:0, one launch (start us, length us, event | category | flops | bytes accessed | tf_op | source)
XLA Modules:
  0.0 93.0 jit_solution(10608358137834040790)
XLA Ops:
  0.6 0.0 copy-start
  0.6 0.8 fusion.22
  1.4 2.3 %reduce-window.6 = s32[8,8,128]{2,1,0:T(8,128)S(1)} reduce-window(s32[8,8,128]{2,1,0:T(8,128)S(1)} %fusion.22, s32[]{:T(128)} %constant.118.clone.1), window={size=1x1x128 pad=0_0x0_0x127_0}, to_apply=%region_0.1 | reduce-window | flops 1040384 | bytes 65540 | tf_op jit(solution)/shard_map/reduce-window
  3.6 0.3 slice_reduce_fusion
  3.9 0.2 reduce-window.9
  4.1 0.1 add_bitcast_fusion
  4.2 0.7 fusion.21
  4.9 0.7 multiply_add_fusion
  5.6 0.7 fusion.25
  6.3 0.7 and_reduce_fusion
  7.1 4.9 %scatter_custom_fusion.2 = s32[4096]{0:T(1024)} fusion(s32[1024]{0:T(1024)S(1)} %broadcast_select_fusion, s32[1024]{0:T(1024)S(1)} %get-tuple-element.25, s32[]{:T(128)} %constant.116.clone.1), kind=kCustom, calls=%fused_computation.79 | custom fusion | bytes 16388
  12.0 5.2 %all-to-all-start = ((s32[1,8,512]{2,0,1:T(1,128)}), s32[1,8,512]{2,0,1:T(1,128)S(1)}, u32[]{:S(2)}, u32[]{:S(2)}) async-start(s32[1,8,512]{2,0,1:T(1,128)} %bitcast.12), calls=%async_computation | async-start | bytes 32768 | tf_op jit(solution)/shard_map/all_to_all | solution.py:77
  17.2 0.9 %copy.91 = f32[5,2,16,128]{3,0,2,1:T(8,128)S(1)} copy(f32[5,2,16,128]{3,2,1,0:T(8,128)} %param.15) | data formatting | bytes 163840 | tf_op args[6]
  18.1 1.3 %collective-permute-start.2 = (f32[5,2,1,128]{3,0,2,1:T(8,128)S(1)}, f32[5,2,1,128]{3,0,2,1:T(8,128)}, u32[]{:S(2)}, u32[]{:S(2)}) collective-permute-start(f32[5,2,1,128]{3,0,2,1:T(8,128)S(1)} %get-tuple-element.13), channel_id=1, source_target_pairs={{1,0},{2,1},{3,2},{5,4},{6,5},{7,6},{9,8},{10,9},{11,10},{13,12},{... | collective-permute-start | bytes 15368 | tf_op jit(solution)/shard_map/ppermute | solution.py:23
  19.4 5.1 %collective-permute-start.3 = (f32[5,2,1,128]{3,0,2,1:T(8,128)S(1)}, f32[5,2,1,128]{3,0,2,1:T(8,128)}, u32[]{:S(2)}, u32[]{:S(2)}) collective-permute-start(f32[5,2,1,128]{3,0,2,1:T(8,128)S(1)} %get-tuple-element.12), channel_id=1, source_target_pairs={{0,1},{1,2},{2,3},{4,5},{5,6},{6,7},{8,9},{9,10},{10,11},{12,13},{... | collective-permute-start | bytes 15368 | tf_op jit(solution)/shard_map/ppermute | solution.py:21
  24.6 0.6 fusion.32
  25.2 2.1 %collective-permute-start = (f32[5,1,16,128]{3,0,2,1:T(8,128)}, f32[5,1,16,128]{3,0,2,1:T(8,128)S(1)}, u32[]{:S(2)}, u32[]{:S(2)}) collective-permute-start(f32[5,1,16,128]{3,0,2,1:T(8,128)} %get-tuple-element.11), channel_id=1, source_target_pairs={{4,0},{8,4},{12,8},{16,12},{20,16},{24,20},{28,24},{0,28},{5,1},{9... | collective-permute-start | bytes 122888 | tf_op jit(solution)/shard_map/ppermute | solution.py:23
  27.3 0.0 collective-permute-start.1
  27.3 0.7 and_compare_fusion.7
  28.0 0.8 slice.95
  28.8 0.0 copy-start.5
  28.8 0.8 pad_select_fusion.6
  29.6 0.1 slice.109
  29.7 0.0 copy-start.1
  29.7 0.9 pad_select_fusion.5
  30.6 0.1 slice.110
  30.7 0.8 pad_select_fusion.4
  31.5 0.1 slice.111
  31.6 0.1 pad_select_fusion.3
  31.7 0.1 slice.112
  31.8 0.1 pad_select_fusion.2
  31.9 0.1 slice.113
  32.0 0.1 pad_select_fusion.1
  32.1 0.1 slice.114
  32.2 0.1 pad_select_fusion
  32.4 0.0 copy-done
  32.4 0.3 convolution_bitcast_fusion
  32.6 0.0 copy-done.5
  32.7 1.1 %fusion.10 = f32[5,2,16,128]{3,0,2,1:T(8,128)} fusion(f32[5,2,16,128]{3,0,2,1:T(8,128)S(1)} %copy.91, f32[1,1,5,5]{3,0,2,1:T(1,128)S(1)} %get-tuple-element.16), kind=kOutput, calls=%fused_computation.16 | convolution fusion | flops 1372160 | bytes 346624 | tf_op jit(solution)/shard_map/kc,karz->carz/dot_general | solution.py:101
  33.7 0.0 copy-done.1
  33.8 0.1 multiply_reduce_fusion
  33.8 17.3 %psum.7 = f32[5,1024]{1,0:T(8,128)S(1)} all-reduce(f32[5,1024]{1,0:T(8,128)S(1)} %multiply_reduce_fusion), channel_id=1, replica_groups=mesh['cells'=8,'obs'=4] {'obs'}, use_global_device_ids=true, to_apply=%region_5.6 | all-reduce | flops 5120 | bytes 40960 | tf_op jit(solution)/shard_map/psum | solution.py:55
  51.2 0.0 copy-start.2
  51.2 0.2 copy.93
  51.4 3.6 %scatter_custom_fusion = f32[5,4096]{0,1:T(8,128)S(1)} fusion(s32[1024]{0:T(1024)S(1)} %get-tuple-element.26, f32[1024,5]{1,0:T(8,128)S(1)} %copy.93, f32[]{:T(128)} %constant.115.clone.1), kind=kCustom, calls=%fused_computation.20 | custom fusion | bytes 81924 | tf_op jit(solution)/shard_map/scatter | solution.py:73
  55.0 1.3 %copy.94 = f32[5,8,512]{2,0,1:T(8,128)} copy(f32[5,8,512]{0,2,1:T(8,128)S(1)} %bitcast.73) | data formatting | bytes 163840 | tf_op jit(solution)/shard_map/all_to_all | solution.py:76
  56.3 0.0 copy-done.2
  56.3 0.0 collective-permute-done.2
  56.3 0.0 collective-permute-done.3
  56.3 1.1 %fusion.9 = f32[5,2,16,128]{3,0,2,1:T(8,128)S(1)} fusion(f32[5,2,1,128]{3,0,2,1:T(8,128)} %collective-permute-done.2, f32[5,2,16,128]{3,0,2,1:T(8,128)S(1)} %copy.91, f32[5,2,1,128]{3,0,2,1:T(8,128)} %collective-permute-done.3, f32[1,1,5,5]{3,0,2,1:T(1,128)S(1)} %get-tuple-element.15), kind=kOutput, calls=%fused_computation.15 | convolution fusion | flops 1454080 | bytes 174180 | tf_op jit(solution)/shard_map/kc,karz->carz/dot_general | solution.py:101
  57.4 0.0 all-to-all-done
  57.4 3.4 %all-to-all-start.1 = ((f32[5,8,512]{2,0,1:T(8,128)}), f32[5,8,512]{2,0,1:T(8,128)S(1)}, u32[]{:S(2)}, u32[]{:S(2)}) async-start(f32[5,8,512]{2,0,1:T(8,128)} %copy.94), calls=%async_computation.1 | async-start | bytes 262144 | tf_op jit(solution)/shard_map/all_to_all | solution.py:76
  60.8 0.5 compare_select_fusion
  61.3 5.0 %all-to-all-done.1 = f32[5,8,512]{2,0,1:T(8,128)S(1)} async-done(((f32[5,8,512]{2,0,1:T(8,128)}), f32[5,8,512]{2,0,1:T(8,128)S(1)}, u32[]{:S(2)}, u32[]{:S(2)}) %all-to-all-start.1) | async-done | bytes 81952 | tf_op jit(solution)/shard_map/all_to_all | solution.py:76
  66.2 2.0 %copy.95 = f32[4096,5]{1,0:T(8,128)} copy(f32[4096,5]{0,1:T(8,128)S(1)} %bitcast.74) | data formatting | bytes 163840 | tf_op jit(solution)/shard_map/all_to_all | solution.py:76
  68.2 0.0 copy-start.3
  68.2 23.2 %scatter_custom_fusion.1 = f32[5,4096]{0,1:T(8,128)S(1)} fusion(s32[4096]{0:T(1024)S(1)} %bitcast.82, f32[4096,5]{1,0:T(8,128)} %copy.95, f32[]{:T(128)} %constant.115.clone.1), kind=kCustom, calls=%fused_computation.18 | custom fusion | flops 20480 | bytes 82432 | tf_op jit(solution)/shard_map/scatter-add | solution.py:88
  91.4 0.6 copy.97
  92.0 0.0 collective-permute-done
  92.0 0.0 collective-permute-done.1
  92.0 0.0 copy-done.3
  92.0 0.0 copy-done.4
  92.0 0.3 fusion.8
  92.4 0.7 copy.98
  (7 shorter events, 0.0 us)
Async XLA Ops:
  0.6 31.7 %copy-start = (bf16[1024,256]{1,0:T(8,128)(2,1)S(1)}, bf16[1024,256]{1,0:T(8,128)(2,1)}, u32[]{:S(2)}) copy-start(bf16[1024,256]{1,0:T(8,128)(2,1)} %param.11) | copy-start | bytes 1572868
  12.0 45.4 %all-to-all-start = ((s32[1,8,512]{2,0,1:T(1,128)}), s32[1,8,512]{2,0,1:T(1,128)S(1)}, u32[]{:S(2)}, u32[]{:S(2)}) async-start(s32[1,8,512]{2,0,1:T(1,128)} %bitcast.12), calls=%async_computation | async-start | bytes 32768 | tf_op jit(solution)/shard_map/all_to_all | solution.py:77
  18.1 38.1 %collective-permute-start.2 = (f32[5,2,1,128]{3,0,2,1:T(8,128)S(1)}, f32[5,2,1,128]{3,0,2,1:T(8,128)}, u32[]{:S(2)}, u32[]{:S(2)}) collective-permute-start(f32[5,2,1,128]{3,0,2,1:T(8,128)S(1)} %get-tuple-element.13), channel_id=1, source_target_pairs={{1,0},{2,1},{3,2},{5,4},{6,5},{7,6},{9,8},{10,9},{11,10},{13,12},{... | collective-permute-start | bytes 15368 | tf_op jit(solution)/shard_map/ppermute | solution.py:23
  19.4 36.9 %collective-permute-start.3 = (f32[5,2,1,128]{3,0,2,1:T(8,128)S(1)}, f32[5,2,1,128]{3,0,2,1:T(8,128)}, u32[]{:S(2)}, u32[]{:S(2)}) collective-permute-start(f32[5,2,1,128]{3,0,2,1:T(8,128)S(1)} %get-tuple-element.12), channel_id=1, source_target_pairs={{0,1},{1,2},{2,3},{4,5},{5,6},{6,7},{8,9},{9,10},{10,11},{12,13},{... | collective-permute-start | bytes 15368 | tf_op jit(solution)/shard_map/ppermute | solution.py:21
  25.2 66.8 %collective-permute-start = (f32[5,1,16,128]{3,0,2,1:T(8,128)}, f32[5,1,16,128]{3,0,2,1:T(8,128)S(1)}, u32[]{:S(2)}, u32[]{:S(2)}) collective-permute-start(f32[5,1,16,128]{3,0,2,1:T(8,128)} %get-tuple-element.11), channel_id=1, source_target_pairs={{4,0},{8,4},{12,8},{16,12},{20,16},{24,20},{28,24},{0,28},{5,1},{9... | collective-permute-start | bytes 122888 | tf_op jit(solution)/shard_map/ppermute | solution.py:23
  27.3 64.7 %collective-permute-start.1 = (f32[5,1,16,128]{3,0,2,1:T(8,128)S(1)}, f32[5,1,16,128]{3,0,2,1:T(8,128)S(1)}, u32[]{:S(2)}, u32[]{:S(2)}) collective-permute-start(f32[5,1,16,128]{3,0,2,1:T(8,128)S(1)} %get-tuple-element.10), channel_id=1, source_target_pairs={{0,4},{4,8},{8,12},{12,16},{16,20},{20,24},{24,28},{28,0},{1,5},{5... | collective-permute-start | bytes 122888 | tf_op jit(solution)/shard_map/ppermute | solution.py:21
  28.8 3.9 %copy-start.5 = (f32[1,3,5,5]{3,0,2,1:T(1,128)S(1)}, f32[1,3,5,5]{3,0,2,1:T(1,128)}, u32[]{:S(2)}) copy-start(f32[1,3,5,5]{3,0,2,1:T(1,128)} %param.17) | copy-start | bytes 904
  29.7 4.0 %copy-start.1 = (bf16[16,5,1024]{2,0,1:T(8,128)(2,1)S(1)}, bf16[16,5,1024]{2,0,1:T(8,128)(2,1)}, u32[]{:S(2)}) copy-start(bf16[16,5,1024]{2,0,1:T(8,128)(2,1)} %param.10) | copy-start | bytes 491524
  51.2 5.1 %copy-start.2 = (f32[5,1024]{1,0:T(8,128)}, f32[5,1024]{1,0:T(8,128)S(1)}, u32[]{:S(2)}) copy-start(f32[5,1024]{1,0:T(8,128)S(1)} %psum.7) | copy-start | bytes 61444
  57.4 8.8 %all-to-all-start.1 = ((f32[5,8,512]{2,0,1:T(8,128)}), f32[5,8,512]{2,0,1:T(8,128)S(1)}, u32[]{:S(2)}, u32[]{:S(2)}) async-start(f32[5,8,512]{2,0,1:T(8,128)} %copy.94), calls=%async_computation.1 | async-start | bytes 262144 | tf_op jit(solution)/shard_map/all_to_all | solution.py:76
  68.2 23.8 %copy-start.3 = (f32[5,2,16,128]{3,0,2,1:T(8,128)S(1)}, f32[5,2,16,128]{3,0,2,1:T(8,128)}, u32[]{:S(2)}) copy-start(f32[5,2,16,128]{3,0,2,1:T(8,128)} %fusion.10) | copy-start | bytes 245764
  68.2 23.8 %copy-start.4 = (f32[2,16,128]{2,1,0:T(8,128)S(1)}, f32[2,16,128]{2,1,0:T(8,128)}, u32[]{:S(2)}) copy-start(f32[2,16,128]{2,1,0:T(8,128)} %param.16) | copy-start | bytes 49156
where the time goes:
time: 94.1 us; the launch traced here: 93 us
  other arithmetic  33.4 us (35%)
  blocking collectives  17.3 us (18%)
  starting transfers between devices  17.1 us (18%)
  local copies, waits for them, and re-layouts  16.5 us (18%)
  waiting for transfers between devices  4.98 us (5%)
  matrix products  2.79 us (3%)
    scatter-add x1, other arithmetic, on_device(): surface = empty_field.at[:, landing].add(received, mode='drop')  23.2 us
    psum x1, blocking collectives, on_device(): panel_source = lax.psum(partial_value, 'obs')  17.3 us
    unnamed x15, local copies, waits for them, and re-layouts  6.53 us
    all_to_all x1, starting transfers between devices, on_device(): lax.all_to_all(out_index, 'cells', split_axis=1, concat_axis=1, tiled=True)  5.2 us
    ppermute x2, starting transfers between devices, extended(): lax.ppermute(tail, axis, [(i, (i + 1) % count) for i in range(ends)])  5.15 us
    all_to_all x1, waiting for transfers between devices, on_device(): lax.all_to_all(outgoing, 'cells', split_axis=1, concat_axis=1, tiled=True)  4.97 us
    scatter x1, local copies, waits for them, and re-layouts, on_device(): jnp.zeros((COMP, devices * capacity), jnp.float32).at[:, slot_of]  3.59 us
    all_to_all x1, starting transfers between devices, on_device(): lax.all_to_all(outgoing, 'cells', split_axis=1, concat_axis=1, tiled=True)  3.38 us
  transfers between devices with their start and end apart: 6, of which 1 were waited for; matrix products, arithmetic and copies ran while one was open for 43% of the time, Pallas kernels for 0%

commit v1 on v0

--- a/solution.py
+++ b/solution.py
@@ -52,7 +52,7 @@
     )
     projected = projected.reshape(projected.shape[0], -1)
     partial_value = jnp.sum(amplitude.astype(jnp.float32) * projected[:, None, :], axis=0)
-    panel_source = lax.psum(partial_value, "obs")
+    panel_source = jnp.sum(lax.all_gather(partial_value, "obs"), axis=0)
     my_block = lax.axis_index("cells")
     my_group = lax.axis_index("obs")
     azimuth_local = adjoint.shape[1]

time: 94.1 us -> 90.5 us (0.962)
  blocking collectives: 17.3 us -> 13.8 us
    psum x1 -> x0, blocking collectives: 17.3 us -> none  [on_device(): panel_source = lax.psum(partial_value, 'obs')]
    all_gather x0 -> x1, blocking collectives: none -> 13.8 us  [on_device(): panel_source = jnp.sum(lax.all_gather(partial_value, 'obs'), axis=0)]
  transfers between devices with their start and end apart: 6 -> 6, of which waited for: 1 -> 1; matrix products, arithmetic and copies ran while one was open for 43% -> 45% of each run, Pallas kernels for 0% -> 0%
where the time goes in v1:
time: 90.5 us; the launch traced here: 89.5 us
  other arithmetic  33.4 us (37%)
  starting transfers between devices  17.1 us (19%)
  local copies, waits for them, and re-layouts  16.5 us (18%)
  blocking collectives  13.8 us (15%)
  waiting for transfers between devices  4.98 us (6%)
  matrix products  2.79 us (3%)
  between operations  0.93 us (1%)
    scatter-add x1, other arithmetic, on_device(): surface = empty_field.at[:, landing].add(received, mode='drop')  23.2 us
    all_gather x1, blocking collectives, on_device(): panel_source = jnp.sum(lax.all_gather(partial_value, 'obs'), axis=0)  13.8 us
    unnamed x15, local copies, waits for them, and re-layouts  6.53 us
    all_to_all x1, starting transfers between devices, on_device(): lax.all_to_all(out_index, 'cells', split_axis=1, concat_axis=1, tiled=True)  5.2 us
    ppermute x2, starting transfers between devices, extended(): lax.ppermute(tail, axis, [(i, (i + 1) % count) for i in range(ends)])  5.15 us
    all_to_all x1, waiting for transfers between devices, on_device(): lax.all_to_all(outgoing, 'cells', split_axis=1, concat_axis=1, tiled=True)  4.97 us
    scatter x1, local copies, waits for them, and re-layouts, on_device(): jnp.zeros((COMP, devices * capacity), jnp.float32).at[:, slot_of]  3.59 us
    all_to_all x1, starting transfers between devices, on_device(): lax.all_to_all(outgoing, 'cells', split_axis=1, concat_axis=1, tiled=True)  3.38 us
  transfers between devices with their start and end apart: 6, of which 1 were waited for; matrix products, arithmetic and copies ran while one was open for 45% of the time, Pallas kernels for 0%

profile of v1, /device:TPU:0, one launch (start us, length us, event | category | flops | bytes accessed | tf_op | source)
XLA Modules:
  0.0 89.5 jit_solution(16178902901365809895)
XLA Ops:
  0.6 0.0 copy-start
  0.6 0.8 fusion.22
  1.4 2.3 %reduce-window.6 = s32[8,8,128]{2,1,0:T(8,128)S(1)} reduce-window(s32[8,8,128]{2,1,0:T(8,128)S(1)} %fusion.22, s32[]{:T(128)} %constant.118.clone.1), window={size=1x1x128 pad=0_0x0_0x127_0}, to_apply=%region_0.1 | reduce-window | flops 1040384 | bytes 65540 | tf_op jit(solution)/shard_map/reduce-window
  3.6 0.3 slice_reduce_fusion
  3.9 0.2 reduce-window.9
  4.1 0.1 add_bitcast_fusion
  4.2 0.7 fusion.21
  4.9 0.7 multiply_add_fusion
  5.6 0.7 fusion.25
  6.3 0.7 and_reduce_fusion
  7.1 4.9 %scatter_custom_fusion.2 = s32[4096]{0:T(1024)} fusion(s32[1024]{0:T(1024)S(1)} %broadcast_select_fusion, s32[1024]{0:T(1024)S(1)} %get-tuple-element.25, s32[]{:T(128)} %constant.116.clone.1), kind=kCustom, calls=%fused_computation.79 | custom fusion | bytes 16388
  12.0 5.2 %all-to-all-start = ((s32[1,8,512]{2,0,1:T(1,128)}), s32[1,8,512]{2,0,1:T(1,128)S(1)}, u32[]{:S(2)}, u32[]{:S(2)}) async-start(s32[1,8,512]{2,0,1:T(1,128)} %bitcast.12), calls=%async_computation | async-start | bytes 32768 | tf_op jit(solution)/shard_map/all_to_all | solution.py:77
  17.2 0.9 %copy.91 = f32[5,2,16,128]{3,0,2,1:T(8,128)S(1)} copy(f32[5,2,16,128]{3,2,1,0:T(8,128)} %param.15) | data formatting | bytes 163840 | tf_op args[6]
  18.1 1.3 %collective-permute-start.2 = (f32[5,2,1,128]{3,0,2,1:T(8,128)S(1)}, f32[5,2,1,128]{3,0,2,1:T(8,128)}, u32[]{:S(2)}, u32[]{:S(2)}) collective-permute-start(f32[5,2,1,128]{3,0,2,1:T(8,128)S(1)} %get-tuple-element.13), channel_id=1, source_target_pairs={{1,0},{2,1},{3,2},{5,4},{6,5},{7,6},{9,8},{10,9},{11,10},{13,12},{... | collective-permute-start | bytes 15368 | tf_op jit(solution)/shard_map/ppermute | solution.py:23
  19.4 5.1 %collective-permute-start.3 = (f32[5,2,1,128]{3,0,2,1:T(8,128)S(1)}, f32[5,2,1,128]{3,0,2,1:T(8,128)}, u32[]{:S(2)}, u32[]{:S(2)}) collective-permute-start(f32[5,2,1,128]{3,0,2,1:T(8,128)S(1)} %get-tuple-element.12), channel_id=1, source_target_pairs={{0,1},{1,2},{2,3},{4,5},{5,6},{6,7},{8,9},{9,10},{10,11},{12,13},{... | collective-permute-start | bytes 15368 | tf_op jit(solution)/shard_map/ppermute | solution.py:21
  24.6 0.6 fusion.32
  25.2 2.1 %collective-permute-start = (f32[5,1,16,128]{3,0,2,1:T(8,128)}, f32[5,1,16,128]{3,0,2,1:T(8,128)S(1)}, u32[]{:S(2)}, u32[]{:S(2)}) collective-permute-start(f32[5,1,16,128]{3,0,2,1:T(8,128)} %get-tuple-element.11), channel_id=1, source_target_pairs={{4,0},{8,4},{12,8},{16,12},{20,16},{24,20},{28,24},{0,28},{5,1},{9... | collective-permute-start | bytes 122888 | tf_op jit(solution)/shard_map/ppermute | solution.py:23
  27.3 0.0 collective-permute-start.1
  27.3 0.7 and_compare_fusion.7
  28.0 0.8 slice.95
  28.8 0.0 copy-start.5
  28.8 0.8 pad_select_fusion.6
  29.6 0.1 slice.109
  29.7 0.0 copy-start.1
  29.7 0.9 pad_select_fusion.5
  30.6 0.1 slice.110
  30.7 0.8 pad_select_fusion.4
  31.5 0.1 slice.111
  31.6 0.1 pad_select_fusion.3
  31.7 0.1 slice.112
  31.8 0.1 pad_select_fusion.2
  31.9 0.1 slice.113
  32.0 0.1 pad_select_fusion.1
  32.1 0.1 slice.114
  32.2 0.1 pad_select_fusion
  32.4 0.0 copy-done
  32.4 0.3 convolution_bitcast_fusion
  32.6 0.0 copy-done.5
  32.7 1.1 %fusion.10 = f32[5,2,16,128]{3,0,2,1:T(8,128)} fusion(f32[5,2,16,128]{3,0,2,1:T(8,128)S(1)} %copy.91, f32[1,1,5,5]{3,0,2,1:T(1,128)S(1)} %get-tuple-element.16), kind=kOutput, calls=%fused_computation.16 | convolution fusion | flops 1372160 | bytes 346624 | tf_op jit(solution)/shard_map/kc,karz->carz/dot_general | solution.py:101
  33.7 0.0 copy-done.1
  33.8 0.1 multiply_reduce_fusion
  33.8 13.8 %all-gather.1 = f32[4,5,1024]{2,1,0:T(8,128)S(1)} all-gather(f32[1,5,1024]{2,1,0:T(8,128)S(1)} %bitcast.78), channel_id=2, replica_groups=mesh['cells'=8,'obs'=4] {'obs'}, dimensions={0}, use_global_device_ids=true | all-gather | bytes 102400 | tf_op jit(solution)/shard_map/all_gather | solution.py:55
  47.6 0.0 copy-start.2
  47.6 0.2 copy.93
  47.8 3.6 %scatter_custom_fusion = f32[5,4096]{0,1:T(8,128)S(1)} fusion(s32[1024]{0:T(1024)S(1)} %get-tuple-element.26, f32[1024,5]{1,0:T(8,128)S(1)} %copy.93, f32[]{:T(128)} %constant.115.clone.1), kind=kCustom, calls=%fused_computation.20 | custom fusion | bytes 81924 | tf_op jit(solution)/shard_map/scatter | solution.py:73
  51.4 1.3 %copy.94 = f32[5,8,512]{2,0,1:T(8,128)} copy(f32[5,8,512]{0,2,1:T(8,128)S(1)} %bitcast.74) | data formatting | bytes 163840 | tf_op jit(solution)/shard_map/all_to_all | solution.py:76
  52.7 0.0 copy-done.2
  52.7 0.0 collective-permute-done.2
  52.7 0.0 collective-permute-done.3
  52.7 1.1 %fusion.9 = f32[5,2,16,128]{3,0,2,1:T(8,128)S(1)} fusion(f32[5,2,1,128]{3,0,2,1:T(8,128)} %collective-permute-done.2, f32[5,2,16,128]{3,0,2,1:T(8,128)S(1)} %copy.91, f32[5,2,1,128]{3,0,2,1:T(8,128)} %collective-permute-done.3, f32[1,1,5,5]{3,0,2,1:T(1,128)S(1)} %get-tuple-element.15), kind=kOutput, calls=%fused_computation.15 | convolution fusion | flops 1454080 | bytes 174180 | tf_op jit(solution)/shard_map/kc,karz->carz/dot_general | solution.py:101
  53.8 0.0 all-to-all-done
  53.8 3.4 %all-to-all-start.1 = ((f32[5,8,512]{2,0,1:T(8,128)}), f32[5,8,512]{2,0,1:T(8,128)S(1)}, u32[]{:S(2)}, u32[]{:S(2)}) async-start(f32[5,8,512]{2,0,1:T(8,128)} %copy.94), calls=%async_computation.1 | async-start | bytes 262144 | tf_op jit(solution)/shard_map/all_to_all | solution.py:76
  57.2 0.5 compare_select_fusion
  57.7 5.0 %all-to-all-done.1 = f32[5,8,512]{2,0,1:T(8,128)S(1)} async-done(((f32[5,8,512]{2,0,1:T(8,128)}), f32[5,8,512]{2,0,1:T(8,128)S(1)}, u32[]{:S(2)}, u32[]{:S(2)}) %all-to-all-start.1) | async-done | bytes 81952 | tf_op jit(solution)/shard_map/all_to_all | solution.py:76
  62.7 2.0 %copy.95 = f32[4096,5]{1,0:T(8,128)} copy(f32[4096,5]{0,1:T(8,128)S(1)} %bitcast.75) | data formatting | bytes 163840 | tf_op jit(solution)/shard_map/all_to_all | solution.py:76
  64.6 0.0 copy-start.3
  64.6 23.2 %scatter_custom_fusion.1 = f32[5,4096]{0,1:T(8,128)S(1)} fusion(s32[4096]{0:T(1024)S(1)} %bitcast.84, f32[4096,5]{1,0:T(8,128)} %copy.95, f32[]{:T(128)} %constant.115.clone.1), kind=kCustom, calls=%fused_computation.18 | custom fusion | flops 20480 | bytes 82432 | tf_op jit(solution)/shard_map/scatter-add | solution.py:88
  87.8 0.6 copy.97
  88.4 0.0 collective-permute-done
  88.4 0.0 collective-permute-done.1
  88.4 0.0 copy-done.3
  88.5 0.0 copy-done.4
  88.5 0.3 fusion.8
  88.8 0.7 copy.98
  (8 shorter events, 0.1 us)
Async XLA Ops:
  0.6 31.7 %copy-start = (bf16[1024,256]{1,0:T(8,128)(2,1)S(1)}, bf16[1024,256]{1,0:T(8,128)(2,1)}, u32[]{:S(2)}) copy-start(bf16[1024,256]{1,0:T(8,128)(2,1)} %param.11) | copy-start | bytes 1572868
  12.0 41.8 %all-to-all-start = ((s32[1,8,512]{2,0,1:T(1,128)}), s32[1,8,512]{2,0,1:T(1,128)S(1)}, u32[]{:S(2)}, u32[]{:S(2)}) async-start(s32[1,8,512]{2,0,1:T(1,128)} %bitcast.12), calls=%async_computation | async-start | bytes 32768 | tf_op jit(solution)/shard_map/all_to_all | solution.py:77
  18.1 34.6 %collective-permute-start.2 = (f32[5,2,1,128]{3,0,2,1:T(8,128)S(1)}, f32[5,2,1,128]{3,0,2,1:T(8,128)}, u32[]{:S(2)}, u32[]{:S(2)}) collective-permute-start(f32[5,2,1,128]{3,0,2,1:T(8,128)S(1)} %get-tuple-element.13), channel_id=1, source_target_pairs={{1,0},{2,1},{3,2},{5,4},{6,5},{7,6},{9,8},{10,9},{11,10},{13,12},{... | collective-permute-start | bytes 15368 | tf_op jit(solution)/shard_map/ppermute | solution.py:23
  19.4 33.3 %collective-permute-start.3 = (f32[5,2,1,128]{3,0,2,1:T(8,128)S(1)}, f32[5,2,1,128]{3,0,2,1:T(8,128)}, u32[]{:S(2)}, u32[]{:S(2)}) collective-permute-start(f32[5,2,1,128]{3,0,2,1:T(8,128)S(1)} %get-tuple-element.12), channel_id=1, source_target_pairs={{0,1},{1,2},{2,3},{4,5},{5,6},{6,7},{8,9},{9,10},{10,11},{12,13},{... | collective-permute-start | bytes 15368 | tf_op jit(solution)/shard_map/ppermute | solution.py:21
  25.2 63.2 %collective-permute-start = (f32[5,1,16,128]{3,0,2,1:T(8,128)}, f32[5,1,16,128]{3,0,2,1:T(8,128)S(1)}, u32[]{:S(2)}, u32[]{:S(2)}) collective-permute-start(f32[5,1,16,128]{3,0,2,1:T(8,128)} %get-tuple-element.11), channel_id=1, source_target_pairs={{4,0},{8,4},{12,8},{16,12},{20,16},{24,20},{28,24},{0,28},{5,1},{9... | collective-permute-start | bytes 122888 | tf_op jit(solution)/shard_map/ppermute | solution.py:23
  27.3 61.1 %collective-permute-start.1 = (f32[5,1,16,128]{3,0,2,1:T(8,128)S(1)}, f32[5,1,16,128]{3,0,2,1:T(8,128)S(1)}, u32[]{:S(2)}, u32[]{:S(2)}) collective-permute-start(f32[5,1,16,128]{3,0,2,1:T(8,128)S(1)} %get-tuple-element.10), channel_id=1, source_target_pairs={{0,4},{4,8},{8,12},{12,16},{16,20},{20,24},{24,28},{28,0},{1,5},{5... | collective-permute-start | bytes 122888 | tf_op jit(solution)/shard_map/ppermute | solution.py:21
  28.8 3.9 %copy-start.5 = (f32[1,3,5,5]{3,0,2,1:T(1,128)S(1)}, f32[1,3,5,5]{3,0,2,1:T(1,128)}, u32[]{:S(2)}) copy-start(f32[1,3,5,5]{3,0,2,1:T(1,128)} %param.17) | copy-start | bytes 904
  29.7 4.0 %copy-start.1 = (bf16[16,5,1024]{2,0,1:T(8,128)(2,1)S(1)}, bf16[16,5,1024]{2,0,1:T(8,128)(2,1)}, u32[]{:S(2)}) copy-start(bf16[16,5,1024]{2,0,1:T(8,128)(2,1)} %param.10) | copy-start | bytes 491524
  47.6 5.1 %copy-start.2 = (f32[5,1024]{1,0:T(8,128)}, f32[5,1024]{1,0:T(8,128)S(1)}, u32[]{:S(2)}) copy-start(f32[5,1024]{1,0:T(8,128)S(1)} %reduce_sum.29) | copy-start | bytes 61444
  53.8 8.8 %all-to-all-start.1 = ((f32[5,8,512]{2,0,1:T(8,128)}), f32[5,8,512]{2,0,1:T(8,128)S(1)}, u32[]{:S(2)}, u32[]{:S(2)}) async-start(f32[5,8,512]{2,0,1:T(8,128)} %copy.94), calls=%async_computation.1 | async-start | bytes 262144 | tf_op jit(solution)/shard_map/all_to_all | solution.py:76
  64.6 23.8 %copy-start.3 = (f32[5,2,16,128]{3,0,2,1:T(8,128)S(1)}, f32[5,2,16,128]{3,0,2,1:T(8,128)}, u32[]{:S(2)}) copy-start(f32[5,2,16,128]{3,0,2,1:T(8,128)} %fusion.10) | copy-start | bytes 245764
  64.6 23.8 %copy-start.4 = (f32[2,16,128]{2,1,0:T(8,128)S(1)}, f32[2,16,128]{2,1,0:T(8,128)}, u32[]{:S(2)}) copy-start(f32[2,16,128]{2,1,0:T(8,128)} %param.16) | copy-start | bytes 49156
